TPU v7x, 32 devices: a whole 2x2x4 slice. The times are simulated.
32 devices in a mesh: parts: 2 (over x), rows: 16 (over z, y, core).
Axes of the slice: x: 2, y: 2, z: 4, core: 2. Of those that a mesh axis runs over, the one named last changes fastest.
Arguments:
- rhs: float32 [3, 12288, 256], P(None, 'rows', 'parts'), parts along dimension 2, may hold values from -6 to 6
- diag_inv: float32 [3, 12288, 768], P(None, 'rows'), may hold values from -0.21875 to 0.21875
- tiles: float32 [2, 32, 768, 768], P(None, 'rows'), may hold values from -0.15625 to 0.15625
- dest: int32 [2, 16, 2], P(None, 'rows'), may hold values from 0 to 15, all different within a row; in each aligned block of 16 rows (0 to 15, 16 to 31, ..., all dimensions but the last counted through in order) at most 4 rows name the same one
- obs_weight: float32 [12288], P('rows'), may hold values from -0.108253175 to 0.108253175, as said below
Outputs:
- solution: float32 [3, 12288, 256], P(None, 'rows', 'parts'), parts along dimension 2
- observed: float32 [256], P('parts'), parts along dimension 0
There are 2 independent parts, one for each index of `parts`. A program takes and returns all parts, laid end to end along the dimension named above; an argument that names none is the same for every part. Nothing has to cross between parts.
Inputs may be any that keep to these rules, and one draw needn't show every extreme that they name: `dest`: in each of the two levels, the two entries of a supernode differ, and no supernode of the next level is named more than 4 times. `obs_weight`: finite weights.
All inputs are finite; a program needn't handle non-finite values.
Results may differ from a plain program's by a relative error of at most 0.00029.
Values sent between devices are 32-bit elements; how exact they have to be, the bound alone decides.
No kernel may reach another device: no remote copies, remote signals or barrier semaphores. Data moves between devices by JAX's collectives and lax.ppermute only.
A program may use at most 128 MiB of HBM per device.

v0:
```python
import jax
import jax.numpy as jnp
from jax import lax
from jax.sharding import PartitionSpec as P


def collect_updates(solved_block, tiles_level, pattern_level):
    products = jnp.einsum(
        "kab,bc->kac",
        tiles_level,
        solved_block,
        precision=lax.Precision.HIGHEST,
        preferred_element_type=jnp.float32,
    )
    block_rows = solved_block.shape[0]
    width = products.shape[2]
    count = lax.axis_size("rows")
    sliced = lax.all_to_all(products, "rows", split_axis=1, concat_axis=0, tiled=True)
    owners = jnp.arange(count, dtype=jnp.int32)
    flat_targets = pattern_level.reshape(-1)
    matches = (owners[:, None] == flat_targets[None, :]).astype(jnp.float32)
    partial_value = jnp.einsum("mq,qac->mac", matches, sliced, precision=lax.Precision.HIGHEST)
    returned = lax.all_to_all(partial_value, "rows", split_axis=0, concat_axis=0, tiled=True)
    return returned.reshape(block_rows, width)


def body(rhs, diag_inv, tiles, dest, obs_weight):
    pattern = lax.all_gather(dest, "rows", axis=1, tiled=True)
    current = rhs[0]
    solved_levels = []
    solved_block = current
    for section in range(3):
        solved_block = jnp.dot(
            diag_inv[section],
            current,
            precision=lax.Precision.HIGHEST,
            preferred_element_type=jnp.float32,
        )
        solved_levels.append(solved_block)
        if section < 2:
            current = rhs[section + 1] - collect_updates(
                solved_block, tiles[section], pattern[section]
            )
    partial_sum = jnp.dot(
        obs_weight,
        solved_block,
        precision=lax.Precision.HIGHEST,
        preferred_element_type=jnp.float32,
    )
    observed = lax.psum(partial_sum, "rows")
    return (jnp.stack(solved_levels), observed)


def solution(mesh):
    in_specs = (
        P(None, "rows", "parts"),
        P(None, "rows", None),
        P(None, "rows", None, None),
        P(None, "rows", None),
        P("rows"),
    )
    out_specs = (P(None, "rows", "parts"), P("parts"))
    return jax.shard_map(body, mesh=mesh, in_specs=in_specs, out_specs=out_specs, check_vma=False)
```

profile of v0, /device:TPU:0, one launch (start us, length us, event | category | flops | bytes accessed | tf_op | source)
XLA Modules:
  0.0 156.5 jit_solution(14306570408259959369)
XLA Ops:
  0.6 3.7 %fusion.10 = f32[768,128]{1,0:T(8,128)S(1)} fusion(f32[3,768,768]{2,1,0:T(8,128)} %param.6, f32[3,768,128]{2,1,0:T(8,128)} %param.5), kind=kOutput, calls=%fused_computation.10 | convolution fusion | flops 905969664 | bytes 3145728 | tf_op jit(solution)/shard_map/dot_general | solution.py:33
  4.3 7.4 %fusion.15 = f32[2,768,128]{1,2,0:T(8,128)S(1)} fusion(f32[2,2,768,768]{3,2,1,0:T(8,128)} %param.7, f32[768,128]{1,0:T(8,128)S(1)} %fusion.10), kind=kOutput, calls=%fused_computation.15 | convolution fusion | flops 1811939328 | bytes 5898240 | tf_op jit(solution)/shard_map/kab,bc->kac/dot_general | solution.py:8
  11.7 0.0 copy-start.3
  11.7 1.2 copy.23
  12.9 0.0 copy-start.1
  12.9 7.5 %all-to-all-start = ((f32[2,768,128]{2,0,1:T(2,128)}), f32[2,768,128]{2,0,1:T(2,128)S(1)}, u32[]{:S(2)}, u32[]{:S(2)}) async-start(f32[2,768,128]{2,0,1:T(2,128)} %copy.23), calls=%async_computation | async-start | bytes 1572864 | tf_op jit(solution)/shard_map/all_to_all | solution.py:18
  20.4 0.0 copy-done.3
  20.4 29.2 %all_gather.3 = s32[2,16,2]{2,0,1:T(2,128)S(1)} all-gather(s32[2,1,2]{2,0,1:T(2,128)S(1)} %bitcast.82), channel_id=1, replica_groups=mesh['parts'=2,'rows'=16] {'rows'}, dimensions={1}, use_global_device_ids=true | all-gather | bytes 272 | tf_op jit(solution)/shard_map/all_gather | solution.py:28
  49.7 0.1 eq.31
  49.8 0.0 all-to-all-done
  49.8 0.0 copy-start
  49.8 0.1 copy.24
  49.8 0.6 copy.25
  50.5 0.4 fusion.29
  50.8 0.1 copy.26
  51.0 16.7 %all_to_all.46 = f32[16,48,128]{2,1,0:T(8,128)S(1)} all-to-all(f32[16,48,128]{2,1,0:T(8,128)S(1)} %copy.26), channel_id=1, replica_groups=mesh['parts'=2,'rows'=16] {'rows'}, dimensions={0} | all-to-all | bytes 786432 | tf_op jit(solution)/shard_map/all_to_all | solution.py:23
  67.7 0.0 copy-done.1
  67.7 0.1 bitcast_subtract_fusion.1
  67.8 3.8 %fusion.8 = f32[128,768]{1,0:T(8,128)S(1)} fusion(f32[3,768,768]{2,1,0:T(8,128)} %param.6, f32[1,768,128]{2,1,0:T(8,128)S(1)} %bitcast_subtract_fusion.1), kind=kOutput, calls=%fused_computation.8 | convolution fusion | flops 905969664 | bytes 3145728 | tf_op jit(solution)/shard_map/dot_general | solution.py:33
  71.5 0.0 copy-done
  71.5 5.0 %fusion.18 = f32[2,768,128]{1,2,0:T(8,128)S(1)} fusion(f32[2,2,768,768]{3,2,1,0:T(8,128)S(1)} %copy-done, f32[128,768]{1,0:T(8,128)S(1)} %fusion.8), kind=kOutput, calls=%fused_computation.16 | convolution fusion | flops 1811939328 | bytes 5898240 | tf_op jit(solution)/shard_map/kab,bc->kac/dot_general | solution.py:8
  76.5 1.2 copy.28
  77.7 3.6 %all-to-all-start.2 = ((f32[2,768,128]{2,0,1:T(2,128)}), f32[2,768,128]{2,0,1:T(2,128)S(1)}, u32[]{:S(2)}, u32[]{:S(2)}) async-start(f32[2,768,128]{2,0,1:T(2,128)} %copy.28), calls=%async_computation.2 | async-start | bytes 1572864 | tf_op jit(solution)/shard_map/all_to_all | solution.py:18
  81.3 0.1 eq.35
  81.4 18.6 %all-to-all-done.2 = f32[2,768,128]{2,0,1:T(2,128)S(1)} async-done(((f32[2,768,128]{2,0,1:T(2,128)}), f32[2,768,128]{2,0,1:T(2,128)S(1)}, u32[]{:S(2)}, u32[]{:S(2)}) %all-to-all-start.2) | async-done | bytes 786464 | tf_op jit(solution)/shard_map/all_to_all | solution.py:18
  99.9 0.1 copy.29
  100.0 0.0 copy-start.2
  100.0 0.6 copy.30
  100.6 0.4 fusion.32
  101.0 0.9 copy.31
  101.9 5.3 %all-to-all-start.3 = ((f32[16,48,128]{2,1,0:T(8,128)}), f32[16,48,128]{2,1,0:T(8,128)S(1)}, u32[]{:S(2)}, u32[]{:S(2)}) async-start(f32[16,48,128]{2,1,0:T(8,128)} %copy.31), calls=%async_computation.3 | async-start | bytes 786432 | tf_op jit(solution)/shard_map/all_to_all | solution.py:23
  107.2 0.0 copy-done.2
  107.3 0.2 copy.27
  107.4 12.0 %all-to-all-done.3 = f32[16,48,128]{2,1,0:T(8,128)S(1)} async-done(((f32[16,48,128]{2,1,0:T(8,128)}), f32[16,48,128]{2,1,0:T(8,128)S(1)}, u32[]{:S(2)}, u32[]{:S(2)}) %all-to-all-start.3) | async-done | bytes 393248 | tf_op jit(solution)/shard_map/all_to_all | solution.py:23
  119.4 3.7 %fusion.6 = f32[128,768]{0,1:T(8,128)S(1)} fusion(f32[3,768,768]{2,1,0:T(8,128)} %param.6, f32[1,768,128]{2,1,0:T(8,128)S(1)} %bitcast_subtract_fusion), kind=kOutput, calls=%fused_computation.6 | convolution fusion | flops 905969664 | bytes 3145728 | tf_op jit(solution)/shard_map/dot_general | solution.py:33
  123.1 0.3 convolution_bitcast_fusion
  123.4 32.0 %psum.7 = f32[128]{0:T(128)} all-reduce(f32[128]{0:T(128)S(1)} %convolution_bitcast_fusion), channel_id=1, replica_groups=mesh['parts'=2,'rows'=16] {'rows'}, use_global_device_ids=true, to_apply=%region_0.0 | all-reduce | flops 128 | bytes 1024 | tf_op jit(solution)/shard_map/psum | solution.py:50
  155.4 1.1 pad_maximum_fusion
  (3 shorter events, 0.1 us)
Async XLA Ops:
  11.7 8.7 %copy-start.3 = (s32[2,1,2]{2,1,0:T(1,128)S(1)}, s32[2,1,2]{2,1,0:T(1,128)}, u32[]{:S(2)}) copy-start(s32[2,1,2]{2,1,0:T(1,128)} %param.8) | copy-start | bytes 52
  12.9 54.8 %copy-start.1 = (f32[3,768,128]{2,1,0:T(8,128)S(1)}, f32[3,768,128]{2,1,0:T(8,128)}, u32[]{:S(2)}) copy-start(f32[3,768,128]{2,1,0:T(8,128)} %param.5) | copy-start | bytes 3538948
  12.9 36.9 %all-to-all-start = ((f32[2,768,128]{2,0,1:T(2,128)}), f32[2,768,128]{2,0,1:T(2,128)S(1)}, u32[]{:S(2)}, u32[]{:S(2)}) async-start(f32[2,768,128]{2,0,1:T(2,128)} %copy.23), calls=%async_computation | async-start | bytes 1572864 | tf_op jit(solution)/shard_map/all_to_all | solution.py:18
  49.8 21.8 %copy-start = (f32[2,2,768,768]{3,2,1,0:T(8,128)S(1)}, f32[2,2,768,768]{3,2,1,0:T(8,128)}, u32[]{:S(2)}) copy-start(f32[2,2,768,768]{3,2,1,0:T(8,128)} %param.7) | copy-start | bytes 28311556
  77.7 22.3 %all-to-all-start.2 = ((f32[2,768,128]{2,0,1:T(2,128)}), f32[2,768,128]{2,0,1:T(2,128)S(1)}, u32[]{:S(2)}, u32[]{:S(2)}) async-start(f32[2,768,128]{2,0,1:T(2,128)} %copy.28), calls=%async_computation.2 | async-start | bytes 1572864 | tf_op jit(solution)/shard_map/all_to_all | solution.py:18
  100.0 7.2 %copy-start.2 = (f32[768]{0:T(1024)S(1)}, f32[768]{0:T(1024)}, u32[]{:S(2)}) copy-start(f32[768]{0:T(1024)} %param.9) | copy-start | bytes 9220
  101.9 17.5 %all-to-all-start.3 = ((f32[16,48,128]{2,1,0:T(8,128)}), f32[16,48,128]{2,1,0:T(8,128)S(1)}, u32[]{:S(2)}, u32[]{:S(2)}) async-start(f32[16,48,128]{2,1,0:T(8,128)} %copy.31), calls=%async_computation.3 | async-start | bytes 786432 | tf_op jit(solution)/shard_map/all_to_all | solution.py:23
where the time goes:
time: 157 us
  blocking collectives  77.9 us (50%)
  waiting for transfers between devices  30.5 us (19%)
  matrix products  24.5 us (16%)
  starting transfers between devices  16.5 us (11%)
  local copies, waits for them, and re-layouts  5.05 us (3%)
    psum x1, blocking collectives, body(): observed = lax.psum(partial_sum, 'rows')  32 us
    all_gather x1, blocking collectives, body(): pattern = lax.all_gather(dest, 'rows', axis=1, tiled=True)  29.2 us
    all_to_all x2, waiting for transfers between devices, collect_updates(): lax.all_to_all(products, 'rows', split_axis=1, concat_axis=0, tiled=True)  18.6 us
    all_to_all x1, blocking collectives, collect_updates(): lax.all_to_all(partial_value, 'rows', split_axis=0, concat_axis=0, tiled=...  16.7 us
    dot_general x2, matrix products, collect_updates(): jnp.einsum('kab,bc->kac', tiles_level, solved_block, precision=lax.Precis...  12.3 us
    all_to_all x1, waiting for transfers between devices, collect_updates(): lax.all_to_all(partial_value, 'rows', split_axis=0, concat_axis=0, tiled=...  12 us
    all_to_all x2, starting transfers between devices, collect_updates(): lax.all_to_all(products, 'rows', split_axis=1, concat_axis=0, tiled=True)  11.2 us
    dot_general x3, matrix products, body(): jnp.dot(diag_inv[section], current, precision=lax.Precision.HIGHEST, pref...  11.1 us
  transfers between devices with their start and end apart: 3, of which 2 were waited for; matrix products, arithmetic and copies ran while one was open for 0% of the time, Pallas kernels for 0%

commit v1 on v0

--- a/solution.py
+++ b/solution.py
@@ -47,7 +47,11 @@
         precision=lax.Precision.HIGHEST,
         preferred_element_type=jnp.float32,
     )
-    observed = lax.psum(partial_sum, "rows")
+    observed = partial_sum
+    for hop in (1, 2, 4, 8):
+        observed = observed + lax.ppermute(
+            observed, "rows", [(dev, dev ^ hop) for dev in range(16)]
+        )
     return (jnp.stack(solved_levels), observed)
 
 

time: 157 us -> 137 us (0.87)
  blocking collectives: 77.9 us -> 45.9 us
  waiting for transfers between devices: 30.5 us -> 38.8 us
  starting transfers between devices: 16.5 us -> 20 us
    psum x1 -> x0, blocking collectives: 32 us -> none  [body(): observed = lax.psum(partial_sum, 'rows')]
    ppermute x0 -> x4, waiting for transfers between devices: none -> 8.08 us  [body(): lax.ppermute(observed, 'rows', [(dev, dev ^ hop) for dev in range(16)])]
    ppermute x0 -> x4, starting transfers between devices: none -> 3.49 us  [body(): lax.ppermute(observed, 'rows', [(dev, dev ^ hop) for dev in range(16)])]
  transfers between devices with their start and end apart: 3 -> 7, of which waited for: 2 -> 6; matrix products, arithmetic and copies ran while one was open for 0% -> 1% of each run, Pallas kernels for 0% -> 0%
where the time goes in v1:
time: 137 us
  blocking collectives  45.9 us (34%)
  waiting for transfers between devices  38.8 us (28%)
  matrix products  24.5 us (18%)
  starting transfers between devices  20 us (15%)
  local copies, waits for them, and re-layouts  5.05 us (4%)
  other arithmetic  1.71 us (1%)
    all_gather x1, blocking collectives, body(): pattern = lax.all_gather(dest, 'rows', axis=1, tiled=True)  29.2 us
    all_to_all x2, waiting for transfers between devices, collect_updates(): lax.all_to_all(products, 'rows', split_axis=1, concat_axis=0, tiled=True)  18.6 us
    all_to_all x1, blocking collectives, collect_updates(): lax.all_to_all(partial_value, 'rows', split_axis=0, concat_axis=0, tiled=...  16.7 us
    dot_general x2, matrix products, collect_updates(): jnp.einsum('kab,bc->kac', tiles_level, solved_block, precision=lax.Precis...  12.3 us
    all_to_all x1, waiting for transfers between devices, collect_updates(): lax.all_to_all(partial_value, 'rows', split_axis=0, concat_axis=0, tiled=...  12.1 us
    all_to_all x2, starting transfers between devices, collect_updates(): lax.all_to_all(products, 'rows', split_axis=1, concat_axis=0, tiled=True)  11.2 us
    dot_general x3, matrix products, body(): jnp.dot(diag_inv[section], current, precision=lax.Precision.HIGHEST, pref...  11.1 us
    ppermute x4, waiting for transfers between devices, body(): lax.ppermute(observed, 'rows', [(dev, dev ^ hop) for dev in range(16)])  8.08 us
  transfers between devices with their start and end apart: 7, of which 6 were waited for; matrix products, arithmetic and copies ran while one was open for 1% of the time, Pallas kernels for 0%

profile of v1, /device:TPU:0, one launch (start us, length us, event | category | flops | bytes accessed | tf_op | source)
XLA Modules:
  0.0 136.8 jit_solution(7946217344844319423)
XLA Ops:
  0.6 3.7 %fusion.10 = f32[768,128]{1,0:T(8,128)S(1)} fusion(f32[3,768,768]{2,1,0:T(8,128)} %param.6, f32[3,768,128]{2,1,0:T(8,128)} %param.5), kind=kOutput, calls=%fused_computation.10 | convolution fusion | flops 905969664 | bytes 3145728 | tf_op jit(solution)/shard_map/dot_general | solution.py:33
  4.3 7.4 %fusion.15 = f32[2,768,128]{1,2,0:T(8,128)S(1)} fusion(f32[2,2,768,768]{3,2,1,0:T(8,128)} %param.7, f32[768,128]{1,0:T(8,128)S(1)} %fusion.10), kind=kOutput, calls=%fused_computation.15 | convolution fusion | flops 1811939328 | bytes 5898240 | tf_op jit(solution)/shard_map/kab,bc->kac/dot_general | solution.py:8
  11.7 0.0 copy-start.3
  11.7 1.2 copy.23
  12.9 0.0 copy-start.1
  12.9 7.5 %all-to-all-start = ((f32[2,768,128]{2,0,1:T(2,128)}), f32[2,768,128]{2,0,1:T(2,128)S(1)}, u32[]{:S(2)}, u32[]{:S(2)}) async-start(f32[2,768,128]{2,0,1:T(2,128)} %copy.23), calls=%async_computation | async-start | bytes 1572864 | tf_op jit(solution)/shard_map/all_to_all | solution.py:18
  20.4 0.0 copy-done.3
  20.4 29.2 %all_gather.3 = s32[2,16,2]{2,0,1:T(2,128)S(1)} all-gather(s32[2,1,2]{2,0,1:T(2,128)S(1)} %bitcast.82), channel_id=1, replica_groups=mesh['parts'=2,'rows'=16] {'rows'}, dimensions={1}, use_global_device_ids=true | all-gather | bytes 272 | tf_op jit(solution)/shard_map/all_gather | solution.py:28
  49.7 0.1 eq.31
  49.8 0.0 all-to-all-done
  49.8 0.0 copy-start
  49.8 0.1 copy.24
  49.8 0.6 copy.25
  50.5 0.4 fusion.29
  50.8 0.1 copy.26
  51.0 16.7 %all_to_all.46 = f32[16,48,128]{2,1,0:T(8,128)S(1)} all-to-all(f32[16,48,128]{2,1,0:T(8,128)S(1)} %copy.26), channel_id=1, replica_groups=mesh['parts'=2,'rows'=16] {'rows'}, dimensions={0} | all-to-all | bytes 786432 | tf_op jit(solution)/shard_map/all_to_all | solution.py:23
  67.7 0.0 copy-done.1
  67.7 0.1 bitcast_subtract_fusion.1
  67.8 3.8 %fusion.8 = f32[128,768]{1,0:T(8,128)S(1)} fusion(f32[3,768,768]{2,1,0:T(8,128)} %param.6, f32[1,768,128]{2,1,0:T(8,128)S(1)} %bitcast_subtract_fusion.1), kind=kOutput, calls=%fused_computation.8 | convolution fusion | flops 905969664 | bytes 3145728 | tf_op jit(solution)/shard_map/dot_general | solution.py:33
  71.5 0.0 copy-done
  71.5 5.0 %fusion.18 = f32[2,768,128]{1,2,0:T(8,128)S(1)} fusion(f32[2,2,768,768]{3,2,1,0:T(8,128)S(1)} %copy-done, f32[128,768]{1,0:T(8,128)S(1)} %fusion.8), kind=kOutput, calls=%fused_computation.16 | convolution fusion | flops 1811939328 | bytes 5898240 | tf_op jit(solution)/shard_map/kab,bc->kac/dot_general | solution.py:8
  76.5 1.2 copy.28
  77.7 3.6 %all-to-all-start.2 = ((f32[2,768,128]{2,0,1:T(2,128)}), f32[2,768,128]{2,0,1:T(2,128)S(1)}, u32[]{:S(2)}, u32[]{:S(2)}) async-start(f32[2,768,128]{2,0,1:T(2,128)} %copy.28), calls=%async_computation.2 | async-start | bytes 1572864 | tf_op jit(solution)/shard_map/all_to_all | solution.py:18
  81.3 0.1 eq.35
  81.4 18.6 %all-to-all-done.2 = f32[2,768,128]{2,0,1:T(2,128)S(1)} async-done(((f32[2,768,128]{2,0,1:T(2,128)}), f32[2,768,128]{2,0,1:T(2,128)S(1)}, u32[]{:S(2)}, u32[]{:S(2)}) %all-to-all-start.2) | async-done | bytes 786464 | tf_op jit(solution)/shard_map/all_to_all | solution.py:18
  99.9 0.1 copy.29
  100.0 0.0 copy-start.2
  100.0 0.6 copy.30
  100.6 0.4 fusion.32
  101.0 0.9 copy.31
  101.9 5.3 %all-to-all-start.3 = ((f32[16,48,128]{2,1,0:T(8,128)}), f32[16,48,128]{2,1,0:T(8,128)S(1)}, u32[]{:S(2)}, u32[]{:S(2)}) async-start(f32[16,48,128]{2,1,0:T(8,128)} %copy.31), calls=%async_computation.3 | async-start | bytes 786432 | tf_op jit(solution)/shard_map/all_to_all | solution.py:23
  107.2 0.0 copy-done.2
  107.3 12.1 %all-to-all-done.3 = f32[16,48,128]{2,1,0:T(8,128)S(1)} async-done(((f32[16,48,128]{2,1,0:T(8,128)}), f32[16,48,128]{2,1,0:T(8,128)S(1)}, u32[]{:S(2)}, u32[]{:S(2)}) %all-to-all-start.3) | async-done | bytes 393248 | tf_op jit(solution)/shard_map/all_to_all | solution.py:23
  119.4 3.7 %fusion.6 = f32[128,768]{0,1:T(8,128)S(1)} fusion(f32[3,768,768]{2,1,0:T(8,128)} %param.6, f32[1,768,128]{2,1,0:T(8,128)S(1)} %bitcast_subtract_fusion), kind=kOutput, calls=%fused_computation.6 | convolution fusion | flops 905969664 | bytes 3145728 | tf_op jit(solution)/shard_map/dot_general | solution.py:33
  123.1 0.3 convolution_bitcast_fusion
  123.4 0.2 collective-permute-start
  123.6 1.0 collective-permute-done
  124.6 0.7 collective-permute-start.1
  125.3 2.9 %collective-permute-done.1 = f32[128]{0:T(128)S(1)} collective-permute-done((f32[128]{0:T(128)S(1)}, f32[128]{0:T(128)S(1)}, u32[]{:S(2)}, u32[]{:S(2)}) %collective-permute-start.1) | collective-permute-done | bytes 544 | tf_op jit(solution)/shard_map/ppermute | solution.py:52
  128.2 0.9 collective-permute-start.2
  129.2 0.2 copy.27
  129.3 2.5 %collective-permute-done.2 = f32[128]{0:T(128)S(1)} collective-permute-done((f32[128]{0:T(128)S(1)}, f32[128]{0:T(128)S(1)}, u32[]{:S(2)}, u32[]{:S(2)}) %collective-permute-start.2) | collective-permute-done | bytes 544 | tf_op jit(solution)/shard_map/ppermute | solution.py:52
  131.8 1.7 %collective-permute-start.3 = (f32[128]{0:T(128)S(1)}, f32[128]{0:T(128)S(1)}, u32[]{:S(2)}, u32[]{:S(2)}) collective-permute-start(f32[128]{0:T(128)S(1)} %add.14), channel_id=1, source_target_pairs={{0,8},{1,9},{2,10},{3,11},{4,12},{5,13},{6,14},{7,15},{8,0},{9,1},... | collective-permute-start | bytes 1544 | tf_op jit(solution)/shard_map/ppermute | solution.py:52
  133.5 1.1 pad_maximum_fusion
  134.6 1.7 %collective-permute-done.3 = f32[128]{0:T(128)S(1)} collective-permute-done((f32[128]{0:T(128)S(1)}, f32[128]{0:T(128)S(1)}, u32[]{:S(2)}, u32[]{:S(2)}) %collective-permute-start.3) | collective-permute-done | bytes 544 | tf_op jit(solution)/shard_map/ppermute | solution.py:52
  136.3 0.5 add.15
  (6 shorter events, 0.1 us)
Async XLA Ops:
  11.7 8.7 %copy-start.3 = (s32[2,1,2]{2,1,0:T(1,128)S(1)}, s32[2,1,2]{2,1,0:T(1,128)}, u32[]{:S(2)}) copy-start(s32[2,1,2]{2,1,0:T(1,128)} %param.8) | copy-start | bytes 52
  12.9 54.8 %copy-start.1 = (f32[3,768,128]{2,1,0:T(8,128)S(1)}, f32[3,768,128]{2,1,0:T(8,128)}, u32[]{:S(2)}) copy-start(f32[3,768,128]{2,1,0:T(8,128)} %param.5) | copy-start | bytes 3538948
  12.9 36.9 %all-to-all-start = ((f32[2,768,128]{2,0,1:T(2,128)}), f32[2,768,128]{2,0,1:T(2,128)S(1)}, u32[]{:S(2)}, u32[]{:S(2)}) async-start(f32[2,768,128]{2,0,1:T(2,128)} %copy.23), calls=%async_computation | async-start | bytes 1572864 | tf_op jit(solution)/shard_map/all_to_all | solution.py:18
  49.8 21.8 %copy-start = (f32[2,2,768,768]{3,2,1,0:T(8,128)S(1)}, f32[2,2,768,768]{3,2,1,0:T(8,128)}, u32[]{:S(2)}) copy-start(f32[2,2,768,768]{3,2,1,0:T(8,128)} %param.7) | copy-start | bytes 28311556
  77.7 22.3 %all-to-all-start.2 = ((f32[2,768,128]{2,0,1:T(2,128)}), f32[2,768,128]{2,0,1:T(2,128)S(1)}, u32[]{:S(2)}, u32[]{:S(2)}) async-start(f32[2,768,128]{2,0,1:T(2,128)} %copy.28), calls=%async_computation.2 | async-start | bytes 1572864 | tf_op jit(solution)/shard_map/all_to_all | solution.py:18
  100.0 7.2 %copy-start.2 = (f32[768]{0:T(1024)S(1)}, f32[768]{0:T(1024)}, u32[]{:S(2)}) copy-start(f32[768]{0:T(1024)} %param.9) | copy-start | bytes 9220
  101.9 17.5 %all-to-all-start.3 = ((f32[16,48,128]{2,1,0:T(8,128)}), f32[16,48,128]{2,1,0:T(8,128)S(1)}, u32[]{:S(2)}, u32[]{:S(2)}) async-start(f32[16,48,128]{2,1,0:T(8,128)} %copy.31), calls=%async_computation.3 | async-start | bytes 786432 | tf_op jit(solution)/shard_map/all_to_all | solution.py:23
  123.4 1.2 collective-permute-start
  124.6 3.6 %collective-permute-start.1 = (f32[128]{0:T(128)S(1)}, f32[128]{0:T(128)S(1)}, u32[]{:S(2)}, u32[]{:S(2)}) collective-permute-start(f32[128]{0:T(128)S(1)} %add.12), channel_id=1, source_target_pairs={{0,2},{1,3},{2,0},{3,1},{4,6},{5,7},{6,4},{7,5},{8,10},{9,11},{10,... | collective-permute-start | bytes 1544 | tf_op jit(solution)/shard_map/ppermute | solution.py:52
  128.2 3.6 %collective-permute-start.2 = (f32[128]{0:T(128)S(1)}, f32[128]{0:T(128)S(1)}, u32[]{:S(2)}, u32[]{:S(2)}) collective-permute-start(f32[128]{0:T(128)S(1)} %add.13), channel_id=1, source_target_pairs={{0,4},{1,5},{2,6},{3,7},{4,0},{5,1},{6,2},{7,3},{8,12},{9,13},{10,... | collective-permute-start | bytes 1544 | tf_op jit(solution)/shard_map/ppermute | solution.py:52
  131.8 4.5 %collective-permute-start.3 = (f32[128]{0:T(128)S(1)}, f32[128]{0:T(128)S(1)}, u32[]{:S(2)}, u32[]{:S(2)}) collective-permute-start(f32[128]{0:T(128)S(1)} %add.14), channel_id=1, source_target_pairs={{0,8},{1,9},{2,10},{3,11},{4,12},{5,13},{6,14},{7,15},{8,0},{9,1},... | collective-permute-start | bytes 1544 | tf_op jit(solution)/shard_map/ppermute | solution.py:52
